TPU v7x, 32 devices: a whole 2x2x4 slice. The times are simulated.
32 devices in a mesh: groups: 2 (over y), block: 4 (over x, core), tensor: 4 (over z).
Axes of the slice: x: 2, y: 2, z: 4, core: 2. Of those that a mesh axis runs over, the one named last changes fastest.
Arguments:
- tokens: bfloat16 [4096, 5120], P(('groups', 'block', 'tensor')), parts along dimension 0, may hold values from -20 to 20
- mod_shift: float32 [5120], replicated, may hold values from -3 to 3
- mod_scale: float32 [5120], replicated, may hold values from -0.5 to 0.5
- w_qkv: bfloat16 [3, 5120, 1024], P(None, 'block', 'tensor'), may hold values from -1 to 1
- tile_list: int32 [8, 4, 5], P(('groups', 'block')), parts along dimension 0, may hold values from 0 to 7, as said below
- tile_count: int32 [8, 4], P(('groups', 'block')), parts along dimension 0, may hold values from 2 to 5, as said below
Outputs:
- attended: bfloat16 [4096, 1024], P(('groups', 'block'), 'tensor'), parts along dimension 0
There are 2 independent parts, one for each index of `groups`. A program takes and returns all parts, laid end to end along the dimension named above; an argument that names none is the same for every part. Nothing has to cross between parts.
Inputs may be any that keep to these rules, and one draw needn't show every extreme that they name: `tile_list`: within the first tile_count[c, t] slots the entries are distinct, the first is the query tile itself (2 + t), and none names a tile outside the slab; blocks at scene cuts name no tile of the block across the cut. Later slots hold indices in range and are not read. `tile_count`: the first query tile of every block reads 5 slots.
All inputs are finite; a program needn't handle non-finite values.
Results may differ from a plain program's by a relative error of at most 0.0087.
Values may be sent and summed in bfloat16 or wider, within the bound.
No kernel may reach another device: no remote copies, remote signals or barrier semaphores. Data moves between devices by JAX's collectives and lax.ppermute only.
A program may use at most 64 MiB of HBM per device.

v0:
```python
import jax
import jax.numpy as jnp
from jax import lax
from jax.sharding import PartitionSpec as P

HEAD_DIM = 128
TILE = 128
BT = 2
epsilon = 1e-06


def with_halo(x, sides, width):
    for axis, dim in sides:
        count, length = (lax.axis_size(axis), x.shape[dim])
        up = [(i, (i + 1) % count) for i in range(count - 1)]
        down = [(j, i) for i, j in up]
        last = lax.slice_in_dim(x, length - width, length, axis=dim)
        first = lax.slice_in_dim(x, 0, width, axis=dim)
        before = lax.ppermute(last, axis, up)
        after = lax.ppermute(first, axis, down)
        x = jnp.concatenate([before, x, after], axis=dim)
    return x


def attend(queries, key_rows, value_rows, chosen_list, chosen_count):
    head_count = queries.shape[1] // HEAD_DIM
    local_tiles = queries.shape[0] // TILE
    all_tiles = key_rows.shape[0] // TILE
    slot_count = chosen_list.shape[1]
    shaped_queries = queries.reshape(local_tiles, TILE, head_count, HEAD_DIM)
    key_tiles = key_rows.reshape(all_tiles, TILE, head_count, HEAD_DIM)[chosen_list]
    value_tiles = value_rows.reshape(all_tiles, TILE, head_count, HEAD_DIM)[chosen_list]
    scores = jnp.einsum(
        "pthd,pkshd->phtks", shaped_queries, key_tiles, preferred_element_type=jnp.float32
    )
    scores = scores * HEAD_DIM ** (-0.5)
    live_slot = jnp.arange(slot_count, dtype=jnp.int32)[None, :] < chosen_count[:, None]
    scores = jnp.where(live_slot[:, None, None, :, None], scores, jnp.float32(-1e30))
    highest = jnp.max(scores, axis=(3, 4), keepdims=True)
    exponent = jnp.exp(scores - highest)
    denominator = jnp.sum(exponent, axis=(3, 4), keepdims=True)
    attn_weights = (exponent / denominator).astype(jnp.bfloat16)
    mixed = jnp.einsum(
        "phtks,pkshd->pthd", attn_weights, value_tiles, preferred_element_type=jnp.float32
    )
    return mixed.astype(jnp.bfloat16).reshape(local_tiles * TILE, head_count * HEAD_DIM)


def shards(tokens, mod_shift, mod_scale, w_qkv, tile_list, tile_count):
    values_in = tokens.astype(jnp.float32)
    row_mean = jnp.mean(values_in, axis=1, keepdims=True)
    centred = values_in - row_mean
    row_var = jnp.mean(centred * centred, axis=1, keepdims=True)
    normed = (centred * lax.rsqrt(row_var + epsilon) * (1.0 + mod_scale) + mod_shift).astype(
        jnp.bfloat16
    )
    gathered = lax.all_gather(normed, "tensor", axis=0, tiled=True)
    projected = jnp.einsum(
        "td,ide->ite",
        gathered,
        lax.all_gather(w_qkv, "block", axis=1, tiled=True),
        preferred_element_type=jnp.float32,
    )
    projected = projected.astype(jnp.bfloat16)
    queries = projected[0]
    key_value = projected[1:3]
    extended = with_halo(key_value, (("block", 1),), BT * TILE)
    return attend(queries, extended[0], extended[1], tile_list[0], tile_count[0])


def solution(mesh):
    return jax.shard_map(
        shards,
        mesh=mesh,
        in_specs=(
            P(("groups", "block", "tensor"), None),
            P(),
            P(),
            P(None, "block", "tensor"),
            P(("groups", "block"), None, None),
            P(("groups", "block"), None),
        ),
        out_specs=P(("groups", "block"), "tensor"),
        check_vma=False,
    )
```

profile of v0, /device:TPU:1, one launch (start us, length us, event | category | flops | bytes accessed | tf_op | source)
XLA Modules:
  0.0 203.5 jit_solution(6897856617463823574)
XLA Ops:
  6.5 0.0 copy-start
  6.5 0.0 copy-start.2
  6.5 0.0 copy-start.1
  6.5 0.0 all-gather.3.cloned.1.call-start
  6.5 1.7 convert_reduce_fusion
  8.2 1.8 fusion.4
  10.1 0.0 copy-done.2
  10.1 0.0 copy-done
  10.1 0.0 copy-done.1
  10.1 0.0 copy-start.3
  10.1 1.7 fusion.7
  11.8 0.0 all-gather.3.cloned.1.call-update
  11.8 0.0 all-gather.5.cloned.1.call-start
  11.9 0.7 all-gather.5.cloned.1.call-update
  12.6 0.0 copy-done.3
  12.6 0.1 reshape.73
  12.7 0.0 copy-start.4
  12.7 99.4 %all-gather.3.cloned.1.call-done = bf16[512,5120]{1,0:T(8,128)(2,1)} async-done(((bf16[128,5120]{1,0:T(8,128)(2,1)}), bf16[512,5120]{1,0:T(8,128)(2,1)}) %all-gather.3.cloned.1.call-update) | async-done | bytes 5242896 | tf_op jit(solution)/shard_map/all_gather | solution.py:57
  112.1 55.6 %all-gather.5.cloned.1.call-done = bf16[3,5120,256]{2,1,0:T(8,128)(2,1)} async-done(((bf16[3,1280,256]{2,1,0:T(8,128)(2,1)}), bf16[3,5120,256]{2,1,0:T(8,128)(2,1)}) %all-gather.5.cloned.1.call-update) | async-done | bytes 7864336 | tf_op jit(solution)/shard_map/all_gather | solution.py:61
  167.7 9.0 %fusion.16 = bf16[3,512,256]{2,1,0:T(8,128)(2,1)S(1)} fusion(bf16[3,5120,256]{2,1,0:T(8,128)(2,1)} %all-gather.5.cloned.1.call-done, bf16[512,5120]{1,0:T(8,128)(2,1)} %all-gather.3.cloned.1.call-done), kind=kOutput, calls=%fused_computation.21 | convolution fusion | flops 4026925056 | bytes 13893632 | tf_op jit(solution)/shard_map/td,ide->ite/dot_general | solution.py:58
  176.7 2.1 %collective-permute-start = (bf16[2,256,256]{2,1,0:T(8,128)(2,1)S(1)}, bf16[2,256,256]{2,1,0:T(8,128)(2,1)S(1)}, u32[]{:S(2)}, u32[]{:S(2)}) collective-permute-start(bf16[2,256,256]{2,1,0:T(8,128)(2,1)S(1)} %get-tuple-element.7), channel_id=1, source_target_pairs={{0,4},{4,8},{8,12},{1,5},{5,9},{9,13},{2,6},{6,10},{10,14},{3,7},{... | collective-permute-start | bytes 786440 | tf_op jit(solution)/shard_map/ppermute | solution.py:19
  178.9 2.2 %collective-permute-start.1 = (bf16[2,256,256]{2,1,0:T(8,128)(2,1)S(1)}, bf16[2,256,256]{2,1,0:T(8,128)(2,1)S(1)}, u32[]{:S(2)}, u32[]{:S(2)}) collective-permute-start(bf16[2,256,256]{2,1,0:T(8,128)(2,1)S(1)} %get-tuple-element.8), channel_id=1, source_target_pairs={{4,0},{8,4},{12,8},{5,1},{9,5},{13,9},{6,2},{10,6},{14,10},{7,3},{... | collective-permute-start | bytes 786440 | tf_op jit(solution)/shard_map/ppermute | solution.py:20
  181.1 0.0 copy-done.4
  181.1 0.1 iota_compare_fusion
  181.3 0.1 reshape_squeeze.10
  181.3 0.8 collective-permute-done
  182.2 4.4 %collective-permute-done.1 = bf16[2,256,256]{2,1,0:T(8,128)(2,1)S(1)} collective-permute-done((bf16[2,256,256]{2,1,0:T(8,128)(2,1)S(1)}, bf16[2,256,256]{2,1,0:T(8,128)(2,1)S(1)}, u32[]{:S(2)}, u32[]{:S(2)}) %collective-permute-start.1) | collective-permute-done | bytes 262176 | tf_op jit(solution)/shard_map/ppermute | solution.py:20
  186.6 0.1 pad_maximum_fusion
  186.6 0.1 fusion.32
  186.7 0.1 reshape_squeeze.11
  186.9 0.1 copy.15
  187.0 0.8 gather_fusion.1
  187.8 0.1 copy.17
  187.9 0.5 fusion.28
  188.4 0.4 fusion.8
  188.8 0.6 fusion.9
  189.4 0.9 reshape_squeeze.9
  190.3 1.1 copy.14
  191.5 1.9 gather_fusion
  193.3 2.4 %fusion.25 = bf16[4,128,2,128]{1,3,2,0:T(8,128)(2,1)S(1)} fusion(f32[4,2,128,5,128]{2,4,3,1,0:T(8,128)S(1)} %bitcast.38, f32[4,2,128]{2,1,0:T(2,128)S(1)} %fusion.9, f32[4,2,128]{2,1,0:T(2,128)S(1)} %fusion.8, pred[4,5]{1,0:T(4,128)(4,1)S(1)} %iota_compare_fusion, bf16[4,5,128,2,128]{4,2,3,1,0:T(8,128)(2,1)} %bitcast.41), kind=kOutput, calls=%fused_computation.24 | convolution fusion | flops 171180032 | bytes 4202516 | tf_op jit(solution)/shard_map/phtks,pkshd->pthd/dot_general | solution.py:43
  195.8 0.2 copy.20
  195.9 0.7 copy.37
  (8 shorter events, 0.1 us)
Async XLA Ops:
  6.5 3.6 %copy-start = (bf16[128,5120]{1,0:T(8,128)(2,1)S(1)}, bf16[128,5120]{1,0:T(8,128)(2,1)}, u32[]{:S(2)}) copy-start(bf16[128,5120]{1,0:T(8,128)(2,1)} %param.6) | copy-start | bytes 3932164
  6.5 3.5 %copy-start.2 = (f32[5120]{0:T(1024)S(1)}, f32[5120]{0:T(1024)}, u32[]{:S(2)}) copy-start(f32[5120]{0:T(1024)} %param.8) | copy-start | bytes 61444
  6.5 3.6 %copy-start.1 = (f32[5120]{0:T(1024)S(1)}, f32[5120]{0:T(1024)}, u32[]{:S(2)}) copy-start(f32[5120]{0:T(1024)} %param.7) | copy-start | bytes 61444
  6.5 105.5 %all-gather.3.cloned.1.call-start = ((), (), s32[]{:S(2)}) async-start(), calls=%async_computation | async-start | bytes 6553600 | tf_op jit(solution)/shard_map/all_gather | solution.py:57
  10.1 2.4 %copy-start.3 = (s32[1,4,5]{2,1,0:T(4,128)S(1)}, s32[1,4,5]{2,1,0:T(4,128)}, u32[]{:S(2)}) copy-start(s32[1,4,5]{2,1,0:T(4,128)} %param.10) | copy-start | bytes 244
  11.8 155.9 %all-gather.5.cloned.1.call-start = ((), (), s32[]{:S(2)}) async-start(), calls=%async_computation.1 | async-start | bytes 9830400 | tf_op jit(solution)/shard_map/all_gather | solution.py:61
  12.7 168.5 %copy-start.4 = (s32[1,4]{1,0:T(1,128)S(1)}, s32[1,4]{1,0:T(1,128)}, u32[]{:S(2)}) copy-start(s32[1,4]{1,0:T(1,128)} %param.11) | copy-start | bytes 52
  176.7 5.4 %collective-permute-start = (bf16[2,256,256]{2,1,0:T(8,128)(2,1)S(1)}, bf16[2,256,256]{2,1,0:T(8,128)(2,1)S(1)}, u32[]{:S(2)}, u32[]{:S(2)}) collective-permute-start(bf16[2,256,256]{2,1,0:T(8,128)(2,1)S(1)} %get-tuple-element.7), channel_id=1, source_target_pairs={{0,4},{4,8},{8,12},{1,5},{5,9},{9,13},{2,6},{6,10},{10,14},{3,7},{... | collective-permute-start | bytes 786440 | tf_op jit(solution)/shard_map/ppermute | solution.py:19
  178.9 7.7 %collective-permute-start.1 = (bf16[2,256,256]{2,1,0:T(8,128)(2,1)S(1)}, bf16[2,256,256]{2,1,0:T(8,128)(2,1)S(1)}, u32[]{:S(2)}, u32[]{:S(2)}) collective-permute-start(bf16[2,256,256]{2,1,0:T(8,128)(2,1)S(1)} %get-tuple-element.8), channel_id=1, source_target_pairs={{4,0},{8,4},{12,8},{5,1},{9,5},{13,9},{6,2},{10,6},{14,10},{7,3},{... | collective-permute-start | bytes 786440 | tf_op jit(solution)/shard_map/ppermute | solution.py:20
Sparse Core Ops, SparseCore 0:
  11.9 100.1 all-gather.2
  113.6 54.0 all-gather.4
where the time goes:
time: 204 us
  waiting for transfers between devices  161 us (79%)
  between operations  13.6 us (7%)
  matrix products  11.9 us (6%)
  other arithmetic  6.35 us (3%)
  local copies, waits for them, and re-layouts  6.3 us (3%)
  starting transfers between devices  4.38 us (2%)
    all_gather x1, waiting for transfers between devices, shards(): gathered = lax.all_gather(normed, 'tensor', axis=0, tiled=True)  99.4 us
    all_gather x1, waiting for transfers between devices, shards(): lax.all_gather(w_qkv, 'block', axis=1, tiled=True)  55.6 us
    dot_general x1, matrix products, shards(): jnp.einsum('td,ide->ite', gathered, lax.all_gather(w_qkv, 'block', axis=1...  9.01 us
    ppermute x1, waiting for transfers between devices, with_halo(): after = lax.ppermute(first, axis, down)  4.4 us
  transfers between devices with their start and end apart: 4, of which 4 were waited for; matrix products, arithmetic and copies ran while one was open for 0% of the time, Pallas kernels for 0%

commit v1 on v0

--- a/solution.py
+++ b/solution.py
@@ -7,6 +7,25 @@
 TILE = 128
 BT = 2
 epsilon = 1e-06
+
+
+def gather_around(x, axis, dim):
+    size, index, rows = (lax.axis_size(axis), lax.axis_index(axis), x.shape[dim])
+    upward = [(i, (i + 1) % size) for i in range(size)]
+    backward = [(i, (i - 1) % size) for i in range(size)]
+    out = jnp.zeros((*x.shape[:dim], size * rows, *x.shape[dim + 1 :]), x.dtype)
+    out = lax.dynamic_update_slice_in_dim(out, x, index * rows, axis=dim)
+    from_left = from_right = x
+    middle = size // 2
+    for hop in range(1, middle + 1):
+        from_left = lax.ppermute(from_left, axis, upward)
+        out = lax.dynamic_update_slice_in_dim(out, from_left, (index - hop) % size * rows, axis=dim)
+        if hop < size - middle:
+            from_right = lax.ppermute(from_right, axis, backward)
+            out = lax.dynamic_update_slice_in_dim(
+                out, from_right, (index + hop) % size * rows, axis=dim
+            )
+    return out
 
 
 def with_halo(x, sides, width):
@@ -54,7 +73,7 @@
     normed = (centred * lax.rsqrt(row_var + epsilon) * (1.0 + mod_scale) + mod_shift).astype(
         jnp.bfloat16
     )
-    gathered = lax.all_gather(normed, "tensor", axis=0, tiled=True)
+    gathered = gather_around(normed, "tensor", 0)
     projected = jnp.einsum(
         "td,ide->ite",
         gathered,

time: 204 us -> 142 us (0.70)
  waiting for transfers between devices: 161 us -> 85.6 us
  local copies, waits for them, and re-layouts: 6.3 us -> 16 us
  starting transfers between devices: 4.38 us -> 12 us
  other arithmetic: 6.35 us -> 2.6 us
    all_gather x1 -> x0, waiting for transfers between devices: 99.4 us -> none  [shards(): gathered = lax.all_gather(normed, 'tensor', axis=0, tiled=True)]
    ppermute x0 -> x3, waiting for transfers between devices: none -> 79.4 us  [the longest x2 52.9 us: gather_around(): from_left = lax.ppermute(from_left, axis, upward)]
    all_gather x1, waiting for transfers between devices: 55.6 us -> 0.01 us  [shards(): lax.all_gather(w_qkv, 'block', axis=1, tiled=True)]
    dynamic_update_slice x0 -> x3, local copies, waits for them, and re-layouts: none -> 6.1 us  [the longest x2 3.66 us: gather_around(): lax.dynamic_update_slice_in_dim(out, from_left, (index - hop) % size * ro...]
    ppermute x0 -> x3, starting transfers between devices: none -> 4.14 us  [the longest x2 2.12 us: gather_around(): from_left = lax.ppermute(from_left, axis, upward)]
    ppermute x1, starting transfers between devices: 2.12 us -> 5.93 us  [with_halo(): before = lax.ppermute(last, axis, up)]
    unnamed x11 -> x13, local copies, waits for them, and re-layouts: 0.76 us -> 3.73 us
  transfers between devices with their start and end apart: 4 -> 6, of which waited for: 4 -> 5; matrix products, arithmetic and copies ran while one was open for 0% -> 6% of each run, Pallas kernels for 0% -> 0%
where the time goes in v1:
time: 142 us
  waiting for transfers between devices  85.6 us (60%)
  local copies, waits for them, and re-layouts  16 us (11%)
  between operations  13.6 us (10%)
  starting transfers between devices  12 us (8%)
  matrix products  11.9 us (8%)
  other arithmetic  2.6 us (2%)
    ppermute x2, waiting for transfers between devices, gather_around(): from_left = lax.ppermute(from_left, axis, upward)  52.9 us
    ppermute x1, waiting for transfers between devices, gather_around(): from_right = lax.ppermute(from_right, axis, backward)  26.5 us
    dot_general x1, matrix products, shards(): jnp.einsum('td,ide->ite', gathered, lax.all_gather(w_qkv, 'block', axis=1...  9.02 us
    ppermute x1, starting transfers between devices, with_halo(): before = lax.ppermute(last, axis, up)  5.93 us
    ppermute x1, waiting for transfers between devices, with_halo(): after = lax.ppermute(first, axis, down)  4.4 us
    unnamed x13, local copies, waits for them, and re-layouts  3.73 us
    dynamic_update_slice x2, local copies, waits for them, and re-layouts, gather_around(): lax.dynamic_update_slice_in_dim(out, from_left, (index - hop) % size * ro...  3.66 us
  transfers between devices with their start and end apart: 6, of which 5 were waited for; matrix products, arithmetic and copies ran while one was open for 6% of the time, Pallas kernels for 0%

profile of v1, /device:TPU:1, one launch (start us, length us, event | category | flops | bytes accessed | tf_op | source)
XLA Modules:
  0.0 141.8 jit_solution(472594483574026436)
XLA Ops:
  6.5 0.0 copy-start
  6.5 0.0 copy-start.3
  6.5 0.0 all-gather.2.cloned.1.call-start
  6.5 0.7 all-gather.2.cloned.1.call-update
  7.3 0.6 copy-done
  7.9 0.3 convert_reduce_fusion
  8.1 0.5 fusion.4
  8.6 0.0 copy-done.3
  8.7 0.0 copy-start.2
  8.7 0.6 broadcast_in_dim.10
  9.3 0.1 copy-done.2
  9.4 0.0 copy-start.4
  9.4 0.6 constant_dynamic-update-slice_fusion.3
  10.0 0.0 copy-start.1
  10.1 2.3 %copy-done.1 = bf16[512,5120]{1,0:T(8,128)(2,1)} copy-done((bf16[512,5120]{1,0:T(8,128)(2,1)}, bf16[512,5120]{1,0:T(8,128)(2,1)S(1)}, u32[]{:S(2)}) %copy-start.1) | copy-done | bytes 5242904
  12.4 2.1 %collective-permute-start = (bf16[128,5120]{1,0:T(8,128)(2,1)S(1)}, bf16[128,5120]{1,0:T(8,128)(2,1)S(1)}, u32[]{:S(2)}, u32[]{:S(2)}) collective-permute-start(bf16[128,5120]{1,0:T(8,128)(2,1)S(1)} %get-tuple-element.6), channel_id=1, source_target_pairs={{0,1},{1,2},{2,3},{3,0},{4,5},{5,6},{6,7},{7,4},{8,9},{9,10},{10,1... | collective-permute-start | bytes 3932168 | tf_op jit(solution)/shard_map/ppermute | solution.py:21
  14.5 2.0 %collective-permute-start.1 = (bf16[128,5120]{1,0:T(8,128)(2,1)S(1)}, bf16[128,5120]{1,0:T(8,128)(2,1)}, u32[]{:S(2)}, u32[]{:S(2)}) collective-permute-start(bf16[128,5120]{1,0:T(8,128)(2,1)S(1)} %get-tuple-element.6), channel_id=1, source_target_pairs={{0,3},{1,0},{2,1},{3,2},{4,7},{5,4},{6,5},{7,6},{8,11},{9,8},{10,9... | collective-permute-start | bytes 3932168 | tf_op jit(solution)/shard_map/ppermute | solution.py:24
  16.5 28.5 %collective-permute-done = bf16[128,5120]{1,0:T(8,128)(2,1)S(1)} collective-permute-done((bf16[128,5120]{1,0:T(8,128)(2,1)S(1)}, bf16[128,5120]{1,0:T(8,128)(2,1)S(1)}, u32[]{:S(2)}, u32[]{:S(2)}) %collective-permute-start) | collective-permute-done | bytes 1310752 | tf_op jit(solution)/shard_map/ppermute | solution.py:21
  45.0 0.0 collective-permute-start.2
  45.0 0.0 copy-done.4
  45.0 0.1 reshape.73
  45.1 1.2 constant_dynamic-update-slice_fusion.2
  46.3 26.5 %collective-permute-done.1 = bf16[128,5120]{1,0:T(8,128)(2,1)} collective-permute-done((bf16[128,5120]{1,0:T(8,128)(2,1)S(1)}, bf16[128,5120]{1,0:T(8,128)(2,1)}, u32[]{:S(2)}, u32[]{:S(2)}) %collective-permute-start.1) | collective-permute-done | bytes 1310752 | tf_op jit(solution)/shard_map/ppermute | solution.py:24
  72.8 2.4 %constant_dynamic-update-slice_fusion.1 = bf16[512,5120]{1,0:T(8,128)(2,1)} fusion(bf16[512,5120]{1,0:T(8,128)(2,1)} %constant_dynamic-update-slice_fusion.2, bf16[128,5120]{1,0:T(8,128)(2,1)} %collective-permute-done.1, s32[]{:T(128)S(6)} %select_n.46), kind=kLoop, calls=%fused_computation.34 | loop fusion | bytes 2621444 | tf_op jit(solution)/shard_map/dynamic_update_slice | solution.py:25
  75.2 24.4 %collective-permute-done.2 = bf16[128,5120]{1,0:T(8,128)(2,1)} collective-permute-done((bf16[128,5120]{1,0:T(8,128)(2,1)S(1)}, bf16[128,5120]{1,0:T(8,128)(2,1)}, u32[]{:S(2)}, u32[]{:S(2)}) %collective-permute-start.2) | collective-permute-done | bytes 1310752 | tf_op jit(solution)/shard_map/ppermute | solution.py:21
  99.6 2.5 %constant_dynamic-update-slice_fusion = bf16[512,5120]{1,0:T(8,128)(2,1)} fusion(bf16[512,5120]{1,0:T(8,128)(2,1)} %constant_dynamic-update-slice_fusion.1, bf16[128,5120]{1,0:T(8,128)(2,1)} %collective-permute-done.2, s32[]{:T(128)S(6)} %select_n.48), kind=kLoop, calls=%fused_computation.33 | loop fusion | bytes 2621444 | tf_op jit(solution)/shard_map/dynamic_update_slice | solution.py:22
  102.1 0.0 copy-start.5
  102.1 0.0 all-gather.2.cloned.1.call-done
  102.1 9.0 %fusion.16 = bf16[3,512,256]{2,1,0:T(8,128)(2,1)S(1)} fusion(bf16[3,5120,256]{2,1,0:T(8,128)(2,1)} %all-gather.2.cloned.1.call-done, bf16[512,5120]{1,0:T(8,128)(2,1)} %constant_dynamic-update-slice_fusion), kind=kOutput, calls=%fused_computation.21 | convolution fusion | flops 4026925056 | bytes 13893632 | tf_op jit(solution)/shard_map/td,ide->ite/dot_general | solution.py:77
  111.2 5.9 %collective-permute-start.3 = (bf16[2,256,256]{2,1,0:T(8,128)(2,1)S(1)}, bf16[2,256,256]{2,1,0:T(8,128)(2,1)S(1)}, u32[]{:S(2)}, u32[]{:S(2)}) collective-permute-start(bf16[2,256,256]{2,1,0:T(8,128)(2,1)S(1)} %get-tuple-element.9), channel_id=1, source_target_pairs={{0,4},{4,8},{8,12},{1,5},{5,9},{9,13},{2,6},{6,10},{10,14},{3,7},{... | collective-permute-start | bytes 786440 | tf_op jit(solution)/shard_map/ppermute | solution.py:38
  117.1 1.9 %collective-permute-start.4 = (bf16[2,256,256]{2,1,0:T(8,128)(2,1)S(1)}, bf16[2,256,256]{2,1,0:T(8,128)(2,1)S(1)}, u32[]{:S(2)}, u32[]{:S(2)}) collective-permute-start(bf16[2,256,256]{2,1,0:T(8,128)(2,1)S(1)} %get-tuple-element.10), channel_id=1, source_target_pairs={{4,0},{8,4},{12,8},{5,1},{9,5},{13,9},{6,2},{10,6},{14,10},{7,3},{... | collective-permute-start | bytes 786440 | tf_op jit(solution)/shard_map/ppermute | solution.py:39
  119.1 0.0 copy-done.5
  119.1 0.1 iota_compare_fusion
  119.2 0.1 reshape_squeeze.10
  119.3 1.1 collective-permute-done.3
  120.4 4.4 %collective-permute-done.4 = bf16[2,256,256]{2,1,0:T(8,128)(2,1)S(1)} collective-permute-done((bf16[2,256,256]{2,1,0:T(8,128)(2,1)S(1)}, bf16[2,256,256]{2,1,0:T(8,128)(2,1)S(1)}, u32[]{:S(2)}, u32[]{:S(2)}) %collective-permute-start.4) | collective-permute-done | bytes 262176 | tf_op jit(solution)/shard_map/ppermute | solution.py:39
  124.8 0.1 pad_maximum_fusion
  124.9 0.1 fusion.33
  125.0 0.1 reshape_squeeze.11
  125.1 0.1 copy.15
  125.2 0.8 gather_fusion.1
  126.0 0.1 copy.17
  126.1 0.5 fusion.28
  126.6 0.4 fusion.8
  127.1 0.6 fusion.9
  127.7 0.9 reshape_squeeze.9
  128.6 1.1 copy.14
  129.7 1.9 %gather_fusion = bf16[20,128,2,128]{3,1,2,0:T(8,128)(2,1)} fusion(bf16[8,128,2,128]{3,1,2,0:T(8,128)(2,1)S(1)} %copy.14, s32[1024]{0:T(1024)S(1)} %pad_clamp_fusion), kind=kCustom, calls=%fused_computation | custom fusion | bytes 2621520 | tf_op jit(solution)/shard_map/gather | solution.py:51
  131.6 2.4 %fusion.25 = bf16[4,128,2,128]{1,3,2,0:T(8,128)(2,1)S(1)} fusion(f32[4,2,128,5,128]{2,4,3,1,0:T(8,128)S(1)} %bitcast.38, f32[4,2,128]{2,1,0:T(2,128)S(1)} %fusion.9, f32[4,2,128]{2,1,0:T(2,128)S(1)} %fusion.8, pred[4,5]{1,0:T(4,128)(4,1)S(1)} %iota_compare_fusion, bf16[4,5,128,2,128]{4,2,3,1,0:T(8,128)(2,1)} %bitcast.41), kind=kOutput, calls=%fused_computation.24 | convolution fusion | flops 171180032 | bytes 4202516 | tf_op jit(solution)/shard_map/phtks,pkshd->pthd/dot_general | solution.py:62
  134.0 0.2 copy.20
  134.2 0.7 copy.37
  (8 shorter events, 0.1 us)
Async XLA Ops:
  6.5 1.3 copy-start
  6.5 2.1 %copy-start.3 = (f32[5120]{0:T(1024)S(1)}, f32[5120]{0:T(1024)}, u32[]{:S(2)}) copy-start(f32[5120]{0:T(1024)} %param.8) | copy-start | bytes 61444
  6.5 95.6 %all-gather.2.cloned.1.call-start = ((), (), s32[]{:S(2)}) async-start(), calls=%async_computation | async-start | bytes 9830400 | tf_op jit(solution)/shard_map/all_gather | solution.py:80
  8.7 0.7 copy-start.2
  9.4 35.6 %copy-start.4 = (s32[1,4,5]{2,1,0:T(4,128)S(1)}, s32[1,4,5]{2,1,0:T(4,128)}, u32[]{:S(2)}) copy-start(s32[1,4,5]{2,1,0:T(4,128)} %param.10) | copy-start | bytes 244
  10.0 2.3 %copy-start.1 = (bf16[512,5120]{1,0:T(8,128)(2,1)}, bf16[512,5120]{1,0:T(8,128)(2,1)S(1)}, u32[]{:S(2)}) copy-start(bf16[512,5120]{1,0:T(8,128)(2,1)S(1)} %get-tuple-element.5) | copy-start | bytes 15728644
  12.4 32.7 %collective-permute-start = (bf16[128,5120]{1,0:T(8,128)(2,1)S(1)}, bf16[128,5120]{1,0:T(8,128)(2,1)S(1)}, u32[]{:S(2)}, u32[]{:S(2)}) collective-permute-start(bf16[128,5120]{1,0:T(8,128)(2,1)S(1)} %get-tuple-element.6), channel_id=1, source_target_pairs={{0,1},{1,2},{2,3},{3,0},{4,5},{5,6},{6,7},{7,4},{8,9},{9,10},{10,1... | collective-permute-start | bytes 3932168 | tf_op jit(solution)/shard_map/ppermute | solution.py:21
  14.5 58.3 %collective-permute-start.1 = (bf16[128,5120]{1,0:T(8,128)(2,1)S(1)}, bf16[128,5120]{1,0:T(8,128)(2,1)}, u32[]{:S(2)}, u32[]{:S(2)}) collective-permute-start(bf16[128,5120]{1,0:T(8,128)(2,1)S(1)} %get-tuple-element.6), channel_id=1, source_target_pairs={{0,3},{1,0},{2,1},{3,2},{4,7},{5,4},{6,5},{7,6},{8,11},{9,8},{10,9... | collective-permute-start | bytes 3932168 | tf_op jit(solution)/shard_map/ppermute | solution.py:24
  45.0 54.6 %collective-permute-start.2 = (bf16[128,5120]{1,0:T(8,128)(2,1)S(1)}, bf16[128,5120]{1,0:T(8,128)(2,1)}, u32[]{:S(2)}, u32[]{:S(2)}) collective-permute-start(bf16[128,5120]{1,0:T(8,128)(2,1)S(1)} %collective-permute-done), channel_id=1, source_target_pairs={{0,1},{1,2},{2,3},{3,0},{4,5},{5,6},{6,7},{7,4},{8,9},{9,10},{10,1... | collective-permute-start | bytes 3932168 | tf_op jit(solution)/shard_map/ppermute | solution.py:21
  102.1 17.0 %copy-start.5 = (s32[1,4]{1,0:T(1,128)S(1)}, s32[1,4]{1,0:T(1,128)}, u32[]{:S(2)}) copy-start(s32[1,4]{1,0:T(1,128)} %param.11) | copy-start | bytes 52
  111.2 9.2 %collective-permute-start.3 = (bf16[2,256,256]{2,1,0:T(8,128)(2,1)S(1)}, bf16[2,256,256]{2,1,0:T(8,128)(2,1)S(1)}, u32[]{:S(2)}, u32[]{:S(2)}) collective-permute-start(bf16[2,256,256]{2,1,0:T(8,128)(2,1)S(1)} %get-tuple-element.9), channel_id=1, source_target_pairs={{0,4},{4,8},{8,12},{1,5},{5,9},{9,13},{2,6},{6,10},{10,14},{3,7},{... | collective-permute-start | bytes 786440 | tf_op jit(solution)/shard_map/ppermute | solution.py:38
  117.1 7.7 %collective-permute-start.4 = (bf16[2,256,256]{2,1,0:T(8,128)(2,1)S(1)}, bf16[2,256,256]{2,1,0:T(8,128)(2,1)S(1)}, u32[]{:S(2)}, u32[]{:S(2)}) collective-permute-start(bf16[2,256,256]{2,1,0:T(8,128)(2,1)S(1)} %get-tuple-element.10), channel_id=1, source_target_pairs={{4,0},{8,4},{12,8},{5,1},{9,5},{13,9},{6,2},{10,6},{14,10},{7,3},{... | collective-permute-start | bytes 786440 | tf_op jit(solution)/shard_map/ppermute | solution.py:39
Sparse Core Ops, SparseCore 0:
  8.9 57.7 all-gather.1
